TPU v7x, 32 devices: a whole 2x2x4 slice. The times are simulated.
32 devices in a mesh: req: 4 (over y, core), seq: 8 (over z, x).
Axes of the slice: x: 2, y: 2, z: 4, core: 2. Of those that a mesh axis runs over, the one named last changes fastest.
Arguments:
- embedded: bfloat16 [4, 48, 3584], P(None, 'req'), may hold values from -6 to 6
- cache_keys: bfloat16 [4, 4096, 2048], P('req', 'seq'), may hold values from -6 to 6
- cache_values: bfloat16 [4, 4096, 2048], P('req', 'seq'), may hold values from -6 to 6
- token_owner: int32 [4, 4096], P('req', 'seq'), may hold values from 0 to 11, as said below
- dealing: int32 [48], replicated, may hold values from 0 to 47, as said below
- lengths: int32 [48], replicated, may hold values from 1 to 2048, as said below
- project_weight: bfloat16 [3584, 8192], P(None, 'seq')
- output_weight: bfloat16 [4096, 3584], P('seq'), may hold values from -0.09375 to 0.09375
- gate_weight: bfloat16 [3584, 14336], P(None, ('req', 'seq')), may hold values from -0.09375 to 0.09375
- up_weight: bfloat16 [3584, 14336], P(None, ('req', 'seq')), may hold values from -0.09375 to 0.09375
- down_weight: bfloat16 [14336, 3584], P(('req', 'seq')), may hold values from -0.046875 to 0.046875
- gain_first: float32 [3584], replicated, may hold values from 0.1 to 1.9
- gain_second: float32 [3584], replicated, may hold values from 0.1 to 1.9
- gain_third: float32 [3584], replicated, may hold values from 0.1 to 1.9
- gain_fourth: float32 [3584], replicated, may hold values from 0.1 to 1.9
Outputs:
- results: bfloat16 [4, 48, 3584], P(None, 'req')
Inputs may be any that keep to these rules, and one draw needn't show every extreme that they name: A permutation of the requests; slot i of req group g serves request dealing[g * 12 + i]. The lengths of the 12 requests dealt to one group sum to 4096; in every group the longest is exactly 2048. `token_owner`: each slot owns a contiguous run of its group's pool, runs in slot order, as many tokens as its request's length.
All inputs are finite; a program needn't handle non-finite values.
Results may differ from a plain program's by a relative error of at most 0.012.
The roundings to bfloat16 on the way count: a program that leaves them out, or rounds other values in their place, can miss the bound.
Values may be sent and summed in bfloat16 or wider, within the bound.
A program may use at most 128 MiB of HBM per device.

v0:
```python
import math
import jax
import jax.numpy as jnp
from jax import lax
from jax.sharding import PartitionSpec as P

H = 16
KVH = 8
HD = 256
STEPS = 4
soft_cap = 50.0
epsilon = 1e-06


def rms_scale(values, gain):
    mean_square = jnp.mean(values * values, axis=-1, keepdims=True)
    return values * lax.rsqrt(mean_square + epsilon) * gain


def rotate(values, positions):
    half_width = values.shape[-1] // 2
    freq_index = jnp.arange(half_width, dtype=jnp.float32)
    inverse = jnp.exp(freq_index * (-2.0 * math.log(10000.0) / values.shape[-1]))
    angles = positions[:, None] * inverse[None, :]
    cosine = jnp.cos(angles)[:, None, :]
    sine = jnp.sin(angles)[:, None, :]
    first_half = values[..., :half_width]
    second_half = values[..., half_width:]
    return jnp.concatenate(
        [first_half * cosine - second_half * sine, second_half * cosine + first_half * sine],
        axis=-1,
    )


def capped_weight(scores):
    return jnp.exp(soft_cap * jnp.tanh(scores / soft_cap))


def rounded(values):
    return lax.optimization_barrier(values.astype(jnp.bfloat16)).astype(jnp.float32)


def body(
    embedded,
    cache_keys,
    cache_values,
    token_owner,
    dealing,
    lengths,
    project_weight,
    output_weight,
    gate_weight,
    up_weight,
    down_weight,
    gain_first,
    gain_second,
    gain_third,
    gain_fourth,
):
    row_count = embedded.shape[1]
    rows = STEPS * row_count
    width = embedded.shape[2]
    local_tokens = cache_keys.shape[1]
    value_width = cache_keys.shape[2]
    group_size = H // KVH
    attention_width = H * HD
    column_count = output_weight.shape[0]
    group_index = lax.axis_index("req")
    seq_index = lax.axis_index("seq")
    seq_size = lax.axis_size("seq")
    req_size = lax.axis_size("req")
    column_start = seq_index * column_count
    slot_requests = lax.dynamic_slice_in_dim(dealing, group_index * row_count, row_count)
    matches = slot_requests[:, None] == jnp.arange(dealing.shape[0], dtype=jnp.int32)[None, :]
    base_positions = jnp.sum(jnp.where(matches, lengths[None, :], 0), axis=1)
    positions = base_positions[None, :] + jnp.arange(STEPS, dtype=jnp.int32)[:, None]
    positions = positions.reshape(rows).astype(jnp.float32)
    key_pool = cache_keys[0].reshape(local_tokens, KVH, HD)
    value_pool = cache_values[0].reshape(local_tokens, KVH, HD)
    slots = jnp.tile(jnp.arange(row_count, dtype=jnp.int32), STEPS)
    moments = jnp.repeat(jnp.arange(STEPS, dtype=jnp.int32), row_count)
    owned_mask = token_owner[0][None, :] == slots[:, None]
    stream = embedded.reshape(rows, width).astype(jnp.float32)
    normed = rms_scale(stream, gain_first).astype(jnp.bfloat16)
    local_part = jnp.dot(normed, project_weight, preferred_element_type=jnp.float32).astype(
        jnp.bfloat16
    )
    projected = lax.all_gather(local_part, "seq", axis=1, tiled=True)
    query_rows = projected[:, :attention_width].astype(jnp.float32).reshape(rows, H, HD)
    queries = (rotate(query_rows, positions) * HD ** (-0.5)).astype(jnp.bfloat16)
    key_rows = (
        projected[:, attention_width : attention_width + value_width]
        .astype(jnp.float32)
        .reshape(rows, KVH, HD)
    )
    fresh_keys = rotate(key_rows, positions).astype(jnp.bfloat16)
    fresh_values = projected[:, attention_width + value_width :].reshape(rows, KVH, HD)
    grouped = queries.reshape(rows, KVH, group_size, HD)
    all_keys = jnp.concatenate([key_pool, fresh_keys], axis=0)
    all_values = jnp.concatenate([value_pool, fresh_values], axis=0)
    fresh_mask = (
        (slots[None, :] == slots[:, None])
        & (moments[None, :] <= moments[:, None])
        & (seq_index == 0)
    )
    mask = jnp.concatenate([owned_mask, fresh_mask], axis=1)
    scores = jnp.einsum("igqd,tgd->igqt", grouped, all_keys, preferred_element_type=jnp.float32)
    weights = jnp.where(mask[:, None, None, :], capped_weight(scores), 0.0)
    totals = lax.psum(jnp.sum(weights, axis=-1), "seq").reshape(rows, H)
    outputs = jnp.einsum(
        "igqt,tgd->igqd",
        weights.astype(jnp.bfloat16),
        all_values,
        preferred_element_type=jnp.float32,
    ).reshape(rows, attention_width)
    outputs = lax.psum_scatter(outputs, "seq", scatter_dimension=1, tiled=True)
    spread = jnp.repeat(totals, HD, axis=1)
    spread = lax.dynamic_slice_in_dim(spread, column_start, column_count, 1)
    attended = (outputs / spread).astype(jnp.bfloat16)
    partial = jnp.dot(attended, output_weight, preferred_element_type=jnp.float32)
    mixed = lax.psum(partial, "seq")
    middle = stream + rms_scale(mixed, gain_second)
    feed_input = rms_scale(middle, gain_third).astype(jnp.bfloat16)
    block_rows = lax.all_gather(feed_input, "req", axis=0, tiled=True)
    gate_part = jnp.dot(block_rows, gate_weight, preferred_element_type=jnp.float32)
    up_part = jnp.dot(block_rows, up_weight, preferred_element_type=jnp.float32)
    hidden = (jax.nn.gelu(gate_part, approximate=True) * up_part).astype(jnp.bfloat16)
    summed = jnp.dot(hidden, down_weight, preferred_element_type=jnp.float32)
    summed = lax.psum_scatter(summed, "req", scatter_dimension=0, tiled=True)
    summed = lax.psum(summed, "seq")
    results = (middle + rms_scale(summed, gain_fourth)).astype(jnp.bfloat16)
    return results.reshape(STEPS, row_count, width)


def solution(mesh):
    return jax.shard_map(
        body,
        mesh=mesh,
        in_specs=(
            P(None, "req", None),
            P("req", "seq", None),
            P("req", "seq", None),
            P("req", "seq"),
            P(),
            P(),
            P(None, "seq"),
            P("seq", None),
            P(None, ("req", "seq")),
            P(None, ("req", "seq")),
            P(("req", "seq"), None),
            P(),
            P(),
            P(),
            P(),
        ),
        out_specs=P(None, "req", None),
        check_vma=False,
    )
```

profile of v0, /device:TPU:0, one launch (start us, length us, event | category | flops | bytes accessed | tf_op | source)
XLA Modules:
  0.0 383.3 jit_solution(17114336762805842567)
XLA Ops:
  6.6 2.1 copy.64
  9.9 2.1 reshape.160
  12.2 4.8 %convolution_convert_fusion = bf16[48,1024]{1,0:T(8,128)(2,1)S(1)} fusion(bf16[3584,1024]{1,0:T(8,128)(2,1)} %param.21, f32[48,3584]{1,0:T(8,128)} %reshape.160, f32[3584]{0:T(1024)S(1)} %copy-done.4, f32[48]{0:T(128)S(1)} %rsqrt.36), kind=kOutput, calls=%fused_computation.14 | convolution fusion | flops 352886784 | bytes 8140992 | tf_op jit(solution)/shard_map/dot_general | solution.py:85
  17.0 33.8 %all_gather.6 = bf16[48,8192]{1,0:T(8,128)(2,1)S(1)} all-gather(bf16[48,1024]{1,0:T(8,128)(2,1)S(1)} %convolution_convert_fusion), channel_id=1, replica_groups=mesh['req'=4,'seq'=8] {'seq'}, dimensions={1}, use_global_device_ids=true | all-gather | bytes 884736 | tf_op jit(solution)/shard_map/all_gather | solution.py:88
  58.6 3.9 %copy.69 = bf16[1,512,2048]{1,2,0:T(8,128)(2,1)} copy(bf16[1,512,2048]{2,1,0:T(8,128)(2,1)} %param.16) | data formatting | bytes 4194304 | tf_op args[1]
  62.6 3.9 %copy.72 = bf16[512,8,256]{2,0,1:T(8,128)(2,1)} copy(bf16[512,8,256]{0,2,1:T(8,128)(2,1)} %bitcast.44) | data formatting | bytes 4194304 | tf_op jit(solution)/shard_map/reshape;squeeze | solution.py:78
  66.5 1.6 copy.92
  68.1 3.9 %copy.65 = bf16[1,512,2048]{1,2,0:T(8,128)(2,1)} copy(bf16[1,512,2048]{2,1,0:T(8,128)(2,1)} %param.17) | data formatting | bytes 4194304 | tf_op args[2]
  72.0 3.9 %copy.67 = bf16[512,8,256]{2,0,1:T(8,128)(2,1)} copy(bf16[512,8,256]{0,2,1:T(8,128)(2,1)} %bitcast.45) | data formatting | bytes 4194304 | tf_op jit(solution)/shard_map/reshape;squeeze | solution.py:79
  77.0 2.9 fusion.40
  80.5 1.5 copy.75
  82.1 2.6 reshape.156
  84.8 21.7 %psum.21 = f32[48,16]{0,1:T(8,128)S(1)} all-reduce(f32[48,16]{0,1:T(8,128)S(1)} %bitcast.56), channel_id=1, replica_groups=mesh['req'=4,'seq'=8] {'seq'}, use_global_device_ids=true, to_apply=%region_4.5 | all-reduce | flops 768 | bytes 6144 | tf_op jit(solution)/shard_map/psum | solution.py:109
  108.1 40.9 %reduce-scatter.3.cloned.1.call-done = f32[48,512]{1,0:T(8,128)} async-done(((f32[48,4096]{1,0:T(8,128)}), f32[48,512]{1,0:T(8,128)}) %reduce-scatter.3.cloned.1.call-update) | async-done | bytes 98320 | tf_op jit(solution)/shard_map/reduce_scatter | solution.py:116
  149.0 3.8 fusion.29
  152.8 72.8 %all-reduce.3.cloned.1.call-done = f32[48,3584]{1,0:T(8,128)} async-done(((f32[48,3584]{1,0:T(8,128)}), f32[48,3584]{1,0:T(8,128)}) %all-reduce.3.cloned.1.call-update) | async-done | bytes 688144 | tf_op jit(solution)/shard_map/psum | solution.py:121
  226.9 1.6 multiply_reduce_fusion.1
  230.3 17.7 %all-gather.2.cloned.1.call-done = bf16[192,3584]{1,0:T(8,128)(2,1)} async-done(((bf16[48,3584]{1,0:T(8,128)(2,1)}), bf16[192,3584]{1,0:T(8,128)(2,1)}) %all-gather.2.cloned.1.call-update) | async-done | bytes 1376272 | tf_op jit(solution)/shard_map/all_gather | solution.py:124
  247.9 4.1 %fusion.41 = f32[192,448]{1,0:T(8,128)} fusion(bf16[192,3584]{1,0:T(8,128)(2,1)} %all-gather.2.cloned.1.call-done, bf16[3584,448]{0,1:T(8,128)(2,1)} %param.23), kind=kOutput, calls=%fused_computation.75 | convolution fusion | flops 616562688 | bytes 4931584 | tf_op jit(solution)/shard_map/dot_general | solution.py:125
  252.1 6.0 %fusion.10 = f32[192,3584]{1,0:T(8,128)} fusion(bf16[448,3584]{1,0:T(8,128)(2,1)S(1)} %copy-done, bf16[192,3584]{1,0:T(8,128)(2,1)} %all-gather.2.cloned.1.call-done, bf16[3584,448]{0,1:T(8,128)(2,1)} %param.24, f32[192,448]{1,0:T(8,128)} %fusion.41), kind=kOutput, calls=%fused_computation.15 | convolution fusion | flops 1233985536 | bytes 10895360 | tf_op jit(solution)/shard_map/dot_general | solution.py:128
  258.2 35.6 %reduce-scatter.5.cloned.1.call-done = f32[48,3584]{1,0:T(8,128)} async-done(((f32[192,3584]{1,0:T(8,128)}), f32[48,3584]{1,0:T(8,128)}) %reduce-scatter.5.cloned.1.call-update) | async-done | bytes 688144 | tf_op jit(solution)/shard_map/reduce_scatter | solution.py:129
  293.8 77.4 %all-reduce.5.cloned.1.call-done = f32[48,3584]{1,0:T(8,128)} async-done(((f32[48,3584]{1,0:T(8,128)}), f32[48,3584]{1,0:T(8,128)}) %all-reduce.5.cloned.1.call-update) | async-done | bytes 688144 | tf_op jit(solution)/shard_map/psum | solution.py:130
  372.4 1.5 add_convert_fusion
  374.7 2.0 copy.77
  (68 shorter events, 17.7 us)
Async XLA Ops:
  6.5 245.5 %copy-start = (bf16[448,3584]{1,0:T(8,128)(2,1)S(1)}, bf16[448,3584]{1,0:T(8,128)(2,1)}, u32[]{:S(2)}) copy-start(bf16[448,3584]{1,0:T(8,128)(2,1)} %param.25) | copy-start | bytes 9633796
  6.5 5.7 %copy-start.4 = (f32[3584]{0:T(1024)S(1)}, f32[3584]{0:T(1024)}, u32[]{:S(2)}) copy-start(f32[3584]{0:T(1024)} %param.26) | copy-start | bytes 43012
  6.5 142.4 %reduce-scatter.3.cloned.1.call-start = ((), (), s32[]{:S(2)}) async-start(), calls=%async_computation.2 | async-start | bytes 884736 | tf_op jit(solution)/shard_map/reduce_scatter | solution.py:116
  17.0 35.6 %copy-start.8 = (s32[48]{0:T(128)S(1)}, s32[48]{0:T(128)}, u32[]{:S(2)}) copy-start(s32[48]{0:T(128)} %param.19) | copy-start | bytes 580
  17.0 35.7 %copy-start.9 = (s32[48]{0:T(128)S(1)}, s32[48]{0:T(128)}, u32[]{:S(2)}) copy-start(s32[48]{0:T(128)} %param.20) | copy-start | bytes 580
  54.9 3.6 copy-start.7
  77.0 2.9 copy-start.2
  77.0 2.9 copy-start.3
  84.7 140.9 %all-reduce.3.cloned.1.call-start = ((), (), s32[]{:S(2)}) async-start(), calls=%async_computation.3 | async-start | bytes 1376256 | tf_op jit(solution)/shard_map/psum | solution.py:121
  149.0 77.9 %copy-start.6 = (f32[3584]{0:T(1024)S(1)}, f32[3584]{0:T(1024)}, u32[]{:S(2)}) copy-start(f32[3584]{0:T(1024)} %param.27) | copy-start | bytes 43012
  152.7 76.6 %copy-start.5 = (f32[3584]{0:T(1024)S(1)}, f32[3584]{0:T(1024)}, u32[]{:S(2)}) copy-start(f32[3584]{0:T(1024)} %param.28) | copy-start | bytes 43012
  152.7 95.2 %all-gather.2.cloned.1.call-start = ((), (), s32[]{:S(2)}) async-start(), calls=%async_computation.4 | async-start | bytes 1720320 | tf_op jit(solution)/shard_map/all_gather | solution.py:124
  228.4 0.9 copy-start.1
  230.2 63.5 %reduce-scatter.5.cloned.1.call-start = ((), (), s32[]{:S(2)}) async-start(), calls=%async_computation.5 | async-start | bytes 3440640 | tf_op jit(solution)/shard_map/reduce_scatter | solution.py:129
  258.1 113.0 %all-reduce.5.cloned.1.call-start = ((), (), s32[]{:S(2)}) async-start(), calls=%async_computation.6 | async-start | bytes 1376256 | tf_op jit(solution)/shard_map/psum | solution.py:130
Sparse Core Ops, SparseCore 0:
  84.8 64.0 reduce-scatter.2
  152.9 72.6 all-reduce.2
  230.3 17.5 all-gather.1
  258.2 35.4 reduce-scatter.4
  297.4 73.6 all-reduce.4
where the time goes:
time: 384 us; the launch traced here: 383 us
  waiting for transfers between devices  244 us (64%)
  blocking collectives  55.5 us (14%)
  local copies, waits for them, and re-layouts  36.6 us (10%)
  matrix products  22.2 us (6%)
  between operations  13.3 us (3%)
  other arithmetic  11.1 us (3%)
    psum x1, waiting for transfers between devices, body(): summed = lax.psum(summed, 'seq')  77.4 us
    psum x1, waiting for transfers between devices, body(): mixed = lax.psum(partial, 'seq')  72.8 us
    reduce_scatter x1, waiting for transfers between devices, body(): outputs = lax.psum_scatter(outputs, 'seq', scatter_dimension=1, tiled=True)  40.9 us
    reduce_scatter x1, waiting for transfers between devices, body(): summed = lax.psum_scatter(summed, 'req', scatter_dimension=0, tiled=True)  35.6 us
    all_gather x1, blocking collectives, body(): projected = lax.all_gather(local_part, 'seq', axis=1, tiled=True)  33.8 us
    psum x1, blocking collectives, body(): totals = lax.psum(jnp.sum(weights, axis=-1), 'seq').reshape(rows, H)  21.7 us
    all_gather x1, waiting for transfers between devices, body(): block_rows = lax.all_gather(feed_input, 'req', axis=0, tiled=True)  17.7 us
    unnamed x26, local copies, waits for them, and re-layouts  12.7 us
  transfers between devices with their start and end apart: 5, of which 5 were waited for; matrix products, arithmetic and copies ran while one was open for 0% of the time, Pallas kernels for 0%

commit v1 on v0

--- a/solution.py
+++ b/solution.py
@@ -121,7 +121,14 @@
     mixed = lax.psum(partial, "seq")
     middle = stream + rms_scale(mixed, gain_second)
     feed_input = rms_scale(middle, gain_third).astype(jnp.bfloat16)
-    block_rows = lax.all_gather(feed_input, "req", axis=0, tiled=True)
+    size = lax.axis_size("req")
+    route = [(i, (i + 1) % size) for i in range(size)]
+    parts = [feed_input]
+    for far in range(1, size):
+        parts = [lax.ppermute(parts[0], "req", route), *parts]
+    whole = jnp.concatenate(parts, axis=0)
+    shift = (lax.axis_index("req") + 1) * parts[-1].shape[0]
+    block_rows = jnp.roll(whole, shift, axis=0)
     gate_part = jnp.dot(block_rows, gate_weight, preferred_element_type=jnp.float32)
     up_part = jnp.dot(block_rows, up_weight, preferred_element_type=jnp.float32)
     hidden = (jax.nn.gelu(gate_part, approximate=True) * up_part).astype(jnp.bfloat16)

time: 384 us -> 389 us (1.013)
  local copies, waits for them, and re-layouts: 36.6 us -> 41.2 us
    ppermute x0 -> x3, waiting for transfers between devices: none -> 20.4 us  [body(): parts = [lax.ppermute(parts[0], 'req', route), *parts]]
    all_gather x1 -> x0, waiting for transfers between devices: 17.7 us -> none  [body(): block_rows = lax.all_gather(feed_input, 'req', axis=0, tiled=True)]
    unnamed x26 -> x44, local copies, waits for them, and re-layouts: 12.7 us -> 18.5 us
  transfers between devices with their start and end apart: 5 -> 7, of which waited for: 5 -> 7; matrix products, arithmetic and copies ran while one was open for 0% -> 0% of each run, Pallas kernels for 0% -> 0%
where the time goes in v1:
time: 389 us; the launch traced here: 388 us
  waiting for transfers between devices  246 us (63%)
  blocking collectives  55.6 us (14%)
  local copies, waits for them, and re-layouts  41.2 us (11%)
  matrix products  19.9 us (5%)
  between operations  13.4 us (3%)
  other arithmetic  11.9 us (3%)
    psum x1, waiting for transfers between devices, body(): summed = lax.psum(summed, 'seq')  77.4 us
    psum x1, waiting for transfers between devices, body(): mixed = lax.psum(partial, 'seq')  72.8 us
    reduce_scatter x1, waiting for transfers between devices, body(): outputs = lax.psum_scatter(outputs, 'seq', scatter_dimension=1, tiled=True)  40.9 us
    reduce_scatter x1, waiting for transfers between devices, body(): summed = lax.psum_scatter(summed, 'req', scatter_dimension=0, tiled=True)  34.6 us
    all_gather x1, blocking collectives, body(): projected = lax.all_gather(local_part, 'seq', axis=1, tiled=True)  33.9 us
    psum x1, blocking collectives, body(): totals = lax.psum(jnp.sum(weights, axis=-1), 'seq').reshape(rows, H)  21.7 us
    ppermute x3, waiting for transfers between devices, body(): parts = [lax.ppermute(parts[0], 'req', route), *parts]  20.4 us
    unnamed x44, local copies, waits for them, and re-layouts  18.5 us
  transfers between devices with their start and end apart: 7, of which 7 were waited for; matrix products, arithmetic and copies ran while one was open for 0% of the time, Pallas kernels for 0%

profile of v1, /device:TPU:0, one launch (start us, length us, event | category | flops | bytes accessed | tf_op | source)
XLA Modules:
  0.0 388.4 jit_solution(3359949737988268971)
XLA Ops:
  7.9 2.0 copy.64
  10.1 2.1 reshape.160
  12.3 4.8 %convolution_convert_fusion = bf16[48,1024]{1,0:T(8,128)(2,1)S(1)} fusion(bf16[3584,1024]{1,0:T(8,128)(2,1)} %param.21, f32[48,3584]{1,0:T(8,128)} %reshape.160, f32[3584]{0:T(1024)S(1)} %copy-done.8, f32[48]{0:T(128)S(1)} %rsqrt.36), kind=kOutput, calls=%fused_computation.16 | convolution fusion | flops 352886784 | bytes 8140992 | tf_op jit(solution)/shard_map/dot_general | solution.py:85
  17.1 33.9 %all_gather.3 = bf16[48,8192]{1,0:T(8,128)(2,1)S(1)} all-gather(bf16[48,1024]{1,0:T(8,128)(2,1)S(1)} %convolution_convert_fusion), channel_id=1, replica_groups=mesh['req'=4,'seq'=8] {'seq'}, dimensions={1}, use_global_device_ids=true | all-gather | bytes 884736 | tf_op jit(solution)/shard_map/all_gather | solution.py:88
  59.4 3.9 %copy.69 = bf16[1,512,2048]{1,2,0:T(8,128)(2,1)} copy(bf16[1,512,2048]{2,1,0:T(8,128)(2,1)} %param.16) | data formatting | bytes 4194304 | tf_op args[1]
  63.3 3.9 %copy.72 = bf16[512,8,256]{2,0,1:T(8,128)(2,1)} copy(bf16[512,8,256]{0,2,1:T(8,128)(2,1)} %bitcast.42) | data formatting | bytes 4194304 | tf_op jit(solution)/shard_map/reshape;squeeze | solution.py:78
  67.2 3.9 %copy.65 = bf16[1,512,2048]{1,2,0:T(8,128)(2,1)} copy(bf16[1,512,2048]{2,1,0:T(8,128)(2,1)} %param.17) | data formatting | bytes 4194304 | tf_op args[2]
  71.1 3.9 %copy.67 = bf16[512,8,256]{2,0,1:T(8,128)(2,1)} copy(bf16[512,8,256]{0,2,1:T(8,128)(2,1)} %bitcast.43) | data formatting | bytes 4194304 | tf_op jit(solution)/shard_map/reshape;squeeze | solution.py:79
  76.1 2.9 fusion.55
  81.1 2.7 reshape.156
  83.8 21.7 %psum.21 = f32[48,16]{0,1:T(8,128)S(1)} all-reduce(f32[48,16]{0,1:T(8,128)S(1)} %bitcast.54), channel_id=1, replica_groups=mesh['req'=4,'seq'=8] {'seq'}, use_global_device_ids=true, to_apply=%region_4.5 | all-reduce | flops 768 | bytes 6144 | tf_op jit(solution)/shard_map/psum | solution.py:109
  107.1 40.9 %reduce-scatter.3.cloned.1.call-done = f32[48,512]{1,0:T(8,128)} async-done(((f32[48,4096]{1,0:T(8,128)}), f32[48,512]{1,0:T(8,128)}) %reduce-scatter.3.cloned.1.call-update) | async-done | bytes 98320 | tf_op jit(solution)/shard_map/reduce_scatter | solution.py:116
  148.0 3.7 fusion.41
  151.8 72.8 %all-reduce.3.cloned.1.call-done = f32[48,3584]{1,0:T(8,128)} async-done(((f32[48,3584]{1,0:T(8,128)}), f32[48,3584]{1,0:T(8,128)}) %all-reduce.3.cloned.1.call-update) | async-done | bytes 688144 | tf_op jit(solution)/shard_map/psum | solution.py:121
  226.0 1.6 multiply_reduce_fusion.1
  228.6 6.7 %collective-permute-done = bf16[48,3584]{1,0:T(8,128)(2,1)S(1)} collective-permute-done((bf16[48,3584]{1,0:T(8,128)(2,1)S(1)}, bf16[48,3584]{1,0:T(8,128)(2,1)S(1)}, u32[]{:S(2)}, u32[]{:S(2)}) %collective-permute-start) | collective-permute-done | bytes 344096 | tf_op jit(solution)/shard_map/ppermute | solution.py:128
  235.3 6.8 %collective-permute-done.1 = bf16[48,3584]{1,0:T(8,128)(2,1)} collective-permute-done((bf16[48,3584]{1,0:T(8,128)(2,1)S(1)}, bf16[48,3584]{1,0:T(8,128)(2,1)}, u32[]{:S(2)}, u32[]{:S(2)}) %collective-permute-start.1) | collective-permute-done | bytes 344096 | tf_op jit(solution)/shard_map/ppermute | solution.py:128
  242.1 7.0 %collective-permute-done.2 = bf16[48,3584]{1,0:T(8,128)(2,1)} collective-permute-done((bf16[48,3584]{1,0:T(8,128)(2,1)}, bf16[48,3584]{1,0:T(8,128)(2,1)}, u32[]{:S(2)}, u32[]{:S(2)}) %collective-permute-start.2) | collective-permute-done | bytes 344096 | tf_op jit(solution)/shard_map/ppermute | solution.py:128
  254.7 1.6 copy-done.4
  256.3 1.8 fusion.9
  258.1 6.1 %fusion.31 = f32[192,3584]{1,0:T(8,128)} fusion(bf16[448,3584]{1,0:T(8,128)(2,1)S(1)} %copy-done, f32[192,448]{1,0:T(8,128)} %fusion.9, bf16[3584,448]{0,1:T(8,128)(2,1)} %param.23, bf16[384,3584]{1,0:T(8,128)(2,1)} %copy-done.4, s32[]{:T(128)S(6)} %select_n.32), kind=kOutput, calls=%fused_computation.38 | convolution fusion | flops 1233985536 | bytes 10944516 | tf_op jit(solution)/shard_map/dot_general | solution.py:135
  264.3 34.6 %reduce-scatter.5.cloned.1.call-done = f32[48,3584]{1,0:T(8,128)} async-done(((f32[192,3584]{1,0:T(8,128)}), f32[48,3584]{1,0:T(8,128)}) %reduce-scatter.5.cloned.1.call-update) | async-done | bytes 688144 | tf_op jit(solution)/shard_map/reduce_scatter | solution.py:136
  298.9 77.4 %all-reduce.5.cloned.1.call-done = f32[48,3584]{1,0:T(8,128)} async-done(((f32[48,3584]{1,0:T(8,128)}), f32[48,3584]{1,0:T(8,128)}) %all-reduce.5.cloned.1.call-update) | async-done | bytes 688144 | tf_op jit(solution)/shard_map/psum | solution.py:137
  379.8 2.0 copy.77
  (91 shorter events, 26.3 us)
Async XLA Ops:
  6.5 251.6 %copy-start = (bf16[448,3584]{1,0:T(8,128)(2,1)S(1)}, bf16[448,3584]{1,0:T(8,128)(2,1)}, u32[]{:S(2)}) copy-start(bf16[448,3584]{1,0:T(8,128)(2,1)} %param.25) | copy-start | bytes 9633796
  6.5 5.7 %copy-start.8 = (f32[3584]{0:T(1024)S(1)}, f32[3584]{0:T(1024)}, u32[]{:S(2)}) copy-start(f32[3584]{0:T(1024)} %param.26) | copy-start | bytes 43012
  6.5 141.5 %reduce-scatter.3.cloned.1.call-start = ((), (), s32[]{:S(2)}) async-start(), calls=%async_computation.2 | async-start | bytes 884736 | tf_op jit(solution)/shard_map/reduce_scatter | solution.py:116
  17.0 35.7 %copy-start.14 = (s32[48]{0:T(128)S(1)}, s32[48]{0:T(128)}, u32[]{:S(2)}) copy-start(s32[48]{0:T(128)} %param.19) | copy-start | bytes 580
  17.0 35.8 %copy-start.15 = (s32[48]{0:T(128)S(1)}, s32[48]{0:T(128)}, u32[]{:S(2)}) copy-start(s32[48]{0:T(128)} %param.20) | copy-start | bytes 580
  17.0 36.3 %copy-start.12 = (s32[1,512]{1,0:T(1,128)S(1)}, s32[1,512]{1,0:T(1,128)}, u32[]{:S(2)}) copy-start(s32[1,512]{1,0:T(1,128)} %param.18) | copy-start | bytes 6148
  76.0 2.9 copy-start.3
  76.1 2.9 copy-start.5
  83.8 140.9 %all-reduce.3.cloned.1.call-start = ((), (), s32[]{:S(2)}) async-start(), calls=%async_computation.3 | async-start | bytes 1376256 | tf_op jit(solution)/shard_map/psum | solution.py:121
  148.0 77.9 %copy-start.9 = (f32[3584]{0:T(1024)S(1)}, f32[3584]{0:T(1024)}, u32[]{:S(2)}) copy-start(f32[3584]{0:T(1024)} %param.27) | copy-start | bytes 43012
  151.8 76.7 %copy-start.6 = (f32[3584]{0:T(1024)S(1)}, f32[3584]{0:T(1024)}, u32[]{:S(2)}) copy-start(f32[3584]{0:T(1024)} %param.28) | copy-start | bytes 43012
  151.8 147.1 %reduce-scatter.5.cloned.1.call-start = ((), (), s32[]{:S(2)}) async-start(), calls=%async_computation.4 | async-start | bytes 3440640 | tf_op jit(solution)/shard_map/reduce_scatter | solution.py:136
  227.6 0.9 copy-start.1
  227.6 14.5 %copy-start.10 = (f32[48]{0:T(128)}, f32[48]{0:T(128)S(1)}, u32[]{:S(2)}) copy-start(f32[48]{0:T(128)S(1)} %add_rsqrt_fusion.2) | copy-start | bytes 580
  228.6 6.7 %collective-permute-start = (bf16[48,3584]{1,0:T(8,128)(2,1)S(1)}, bf16[48,3584]{1,0:T(8,128)(2,1)S(1)}, u32[]{:S(2)}, u32[]{:S(2)}) collective-permute-start(bf16[48,3584]{1,0:T(8,128)(2,1)S(1)} %multiply_convert_fusion), channel_id=1, source_target_pairs={{0,8},{8,16},{16,24},{24,0},{1,9},{9,17},{17,25},{25,1},{2,10},{10... | collective-permute-start | bytes 1032200 | tf_op jit(solution)/shard_map/ppermute | solution.py:128
  235.3 6.8 %collective-permute-start.1 = (bf16[48,3584]{1,0:T(8,128)(2,1)S(1)}, bf16[48,3584]{1,0:T(8,128)(2,1)}, u32[]{:S(2)}, u32[]{:S(2)}) collective-permute-start(bf16[48,3584]{1,0:T(8,128)(2,1)S(1)} %collective-permute-done), channel_id=1, source_target_pairs={{0,8},{8,16},{16,24},{24,0},{1,9},{9,17},{17,25},{25,1},{2,10},{10... | collective-permute-start | bytes 1032200 | tf_op jit(solution)/shard_map/ppermute | solution.py:128
  242.1 7.0 %collective-permute-start.2 = (bf16[48,3584]{1,0:T(8,128)(2,1)}, bf16[48,3584]{1,0:T(8,128)(2,1)}, u32[]{:S(2)}, u32[]{:S(2)}) collective-permute-start(bf16[48,3584]{1,0:T(8,128)(2,1)} %collective-permute-done.1), channel_id=1, source_target_pairs={{0,8},{8,16},{16,24},{24,0},{1,9},{9,17},{17,25},{25,1},{2,10},{10... | collective-permute-start | bytes 1032200 | tf_op jit(solution)/shard_map/ppermute | solution.py:128
  242.1 12.5 %copy-start.2 = (f32[48,3584]{1,0:T(8,128)S(1)}, f32[48,3584]{1,0:T(8,128)}, u32[]{:S(2)}) copy-start(f32[48,3584]{1,0:T(8,128)} %copy-done.1) | copy-start | bytes 2064388
  242.1 12.5 %copy-start.7 = (f32[3584]{0:T(1024)S(1)}, f32[3584]{0:T(1024)}, u32[]{:S(2)}) copy-start(f32[3584]{0:T(1024)} %param.28) | copy-start | bytes 43012
  242.1 12.5 %copy-start.11 = (f32[48]{0:T(128)S(1)}, f32[48]{0:T(128)}, u32[]{:S(2)}) copy-start(f32[48]{0:T(128)} %copy-done.10) | copy-start | bytes 580
  250.1 6.2 %copy-start.13 = (bf16[3584,448]{0,1:T(8,128)(2,1)S(1)}, bf16[3584,448]{0,1:T(8,128)(2,1)}, u32[]{:S(2)}) copy-start(bf16[3584,448]{0,1:T(8,128)(2,1)} %param.24) | copy-start | bytes 9633796
  254.7 1.6 copy-start.4
  264.2 112.0 %all-reduce.5.cloned.1.call-start = ((), (), s32[]{:S(2)}) async-start(), calls=%async_computation.5 | async-start | bytes 1376256 | tf_op jit(solution)/shard_map/psum | solution.py:137
Sparse Core Ops, SparseCore 0:
  83.9 64.0 reduce-scatter.2
  151.9 72.7 all-reduce.2
  264.4 34.4 reduce-scatter.4
  302.5 73.6 all-reduce.4
